TPU v7x, 32 devices: a whole 2x2x4 slice. The times are simulated.
32 devices in a mesh: px: 8 (over z, y), py: 4 (over x, core).
Axes of the slice: x: 2, y: 2, z: 4, core: 2. Of those that a mesh axis runs over, the one named last changes fastest.
Arguments:
- spectrum: float32 [2, 1536, 24576], P(None, 'px', 'py'), may hold values from -6 to 6
- concentration: float32 [3072, 24576], P('px', 'py'), may hold values from -6 to 6
- factor_y: float32 [1536, 128], P('py'), may hold values from -0.15625 to 0.15625
- factor_x: float32 [3072, 256], P('px'), may hold values from -0.109375 to 0.109375
Outputs:
- y_compressed: float32 [16, 3072, 128], P('py', 'px')
- core_tensor: float32 [16, 256, 128], P('py', 'px')
All inputs are finite; a program needn't handle non-finite values.
Results may differ from a plain program's by a relative error of at most 0.000076.
Values sent between devices are 32-bit elements; how exact they have to be, the bound alone decides.
No kernel may reach another device: no remote copies, remote signals or barrier semaphores. Data moves between devices by JAX's collectives and lax.ppermute only.
A program may use at most 128 MiB of HBM per device.

v0:
```python
import math
import jax
import jax.numpy as jnp
from jax import lax
from jax.sharding import PartitionSpec as P

NX = 3072
NZ = 16
KX = 1536


def synth_table(first_x, block_width):
    wave = lax.broadcasted_iota(jnp.int32, (KX, block_width), 0)
    column = first_x + lax.broadcasted_iota(jnp.int32, (KX, block_width), 1)
    phase = wave * column % NX
    angle = phase.astype(jnp.float32) * (2.0 * math.pi / NX)
    weight = jnp.where(wave == 0, 1.0, 2.0) / math.sqrt(KX)
    return jnp.concatenate([weight * jnp.cos(angle), -weight * jnp.sin(angle)], axis=0)


def body(spectrum, concentration, factor_y, factor_x):
    x_local = concentration.shape[0]
    line_total = concentration.shape[1]
    y_local = line_total // NZ
    pencil_modes = lax.all_to_all(spectrum, "px", split_axis=2, concat_axis=1, tiled=True)
    line_count = pencil_modes.shape[2]
    stacked_modes = pencil_modes.reshape(2 * KX, line_count)
    block_width = 512
    block_total = NX // block_width

    def fill_block(block_index, velocity):
        first_x = block_index * block_width
        rows = lax.dot_general(
            synth_table(first_x, block_width),
            stacked_modes,
            (((0,), (0,)), ((), ())),
            precision=lax.Precision.HIGHEST,
            preferred_element_type=jnp.float32,
        )
        return lax.dynamic_update_slice_in_dim(velocity, rows, first_x, 0)

    velocity = lax.fori_loop(0, block_total, fill_block, jnp.zeros((NX, line_count), jnp.float32))
    returned = lax.all_to_all(velocity, "px", split_axis=0, concat_axis=1, tiled=True)
    flux_tile = returned * concentration
    flux_cube = flux_tile.reshape(x_local, y_local, NZ)
    rows = flux_cube
    y_compressed = lax.psum_scatter(
        jnp.einsum("xyz,yr->zxr", rows, factor_y, precision=lax.Precision.HIGHEST),
        "py",
        scatter_dimension=0,
        tiled=True,
    )
    core_terms = jnp.einsum("xs,zxr->zsr", factor_x, y_compressed, precision=lax.Precision.HIGHEST)
    core_tensor = lax.psum_scatter(core_terms, "px", scatter_dimension=1, tiled=True)
    return (y_compressed, core_tensor)


def solution(mesh):
    placed = (P(None, "px", "py"), P("px", "py"), P("py", None), P("px", None))
    return jax.shard_map(
        body,
        mesh=mesh,
        in_specs=placed,
        out_specs=(P("py", "px", None), P("py", "px", None)),
        check_vma=False,
    )
```

profile of v0, /device:TPU:0, one launch (start us, length us, event | category | flops | bytes accessed | tf_op | source)
XLA Modules:
  0.0 983.5 jit_solution(7462423224211802599)
XLA Ops:
  7.2 0.0 copy-start
  7.2 18.4 %copy.17 = f32[2,192,6144]{1,0,2:T(2,128)} copy(f32[2,192,6144]{2,1,0:T(8,128)} %param.6) | data formatting | bytes 18874368 | tf_op args[0]
  25.6 7.3 all-to-all-start
  32.9 273.1 %all-to-all-done = f32[2,192,6144]{1,0,2:T(2,128)} async-done(((f32[2,192,6144]{1,0,2:T(2,128)}), f32[2,192,6144]{1,0,2:T(2,128)}, u32[]{:S(2)}, u32[]{:S(2)}) %all-to-all-start) | async-done | bytes 9437216 | tf_op jit(solution)/shard_map/all_to_all | solution.py:25
  306.0 18.3 %copy.18 = f32[2,8,192,768]{3,2,1,0:T(8,128)} copy(f32[2,8,192,768]{2,0,3,1:T(2,128)} %bitcast.1) | data formatting | bytes 18874368 | tf_op jit(solution)/shard_map/all_to_all | solution.py:25
  324.3 4.2 broadcast_in_dim.15
  328.5 281.5 %while.15 = (s32[]{:T(128)}, f32[3072,768]{1,0:T(8,128)}, f32[3072,768]{1,0:T(8,128)}, s32[]{:T(128)}, s32[]{:T(128)}, /*index=5*/s32[]{:T(128)}, s32[]{:T(128)}) while((s32[]{:T(128)}, f32[3072,768]{1,0:T(8,128)}, f32[3072,768]{1,0:T(8,128)}, s32[]{:T(128)}, s32[]{:T(128)}, /*index=5*/s32[]{:T(128)}, s32[]{:T(128)}) %tuple.56), condition=%wide.region_1.2_spmd, body=%wide.region_0.1_spmd.sunk | while | flops 14505745408 | bytes 23621764 | solution.py:42
  328.5 13.5 %cosine_multiply_fusion.2 = (f32[1536,512]{1,0:T(8,128)S(1)}, f32[1536,512]{1,0:T(8,128)S(1)}) fusion(s32[512]{0:T(512)S(1)} %iota_add_fusion.2, f32[1536]{0:T(1024)S(1)} %get-tuple-element.131, f32[1536]{0:T(1024)S(1)} %get-tuple-element.132), kind=kLoop, calls=%fused_computation.8.clone.1 | loop fusion | flops 8650752 | bytes 6305792 | tf_op jit(solution)/shard_map/while/body/eval_jaxpr/mul | solution.py:18
  342.1 33.4 %fusion.28 = f32[3072,768]{1,0:T(8,128)} fusion(f32[3072,768]{1,0:T(8,128)} %get-tuple-element.143, s32[]{:T(128)S(6)} %select_n.61, f32[3072,768]{1,0:T(8,128)} %get-tuple-element.151, f32[1536,512]{1,0:T(8,128)S(1)} %get-tuple-element.133, f32[1536,512]{1,0:T(8,128)S(1)} %get-tuple-element.134), kind=kOutput, calls=%fused_computation.13.clone.1 | convolution fusion | flops 14497087488 | bytes 17301508 | tf_op jit(solution)/shard_map/while/body/eval_jaxpr/dot_general | solution.py:33
  375.4 13.5 %cosine_multiply_fusion.2 = (f32[1536,512]{1,0:T(8,128)S(1)}, f32[1536,512]{1,0:T(8,128)S(1)}) fusion(s32[512]{0:T(512)S(1)} %iota_add_fusion.2, f32[1536]{0:T(1024)S(1)} %get-tuple-element.131, f32[1536]{0:T(1024)S(1)} %get-tuple-element.132), kind=kLoop, calls=%fused_computation.8.clone.1 | loop fusion | flops 8650752 | bytes 6305792 | tf_op jit(solution)/shard_map/while/body/eval_jaxpr/mul | solution.py:18
  388.9 33.4 %fusion.28 = f32[3072,768]{1,0:T(8,128)} fusion(f32[3072,768]{1,0:T(8,128)} %get-tuple-element.143, s32[]{:T(128)S(6)} %select_n.61, f32[3072,768]{1,0:T(8,128)} %get-tuple-element.151, f32[1536,512]{1,0:T(8,128)S(1)} %get-tuple-element.133, f32[1536,512]{1,0:T(8,128)S(1)} %get-tuple-element.134), kind=kOutput, calls=%fused_computation.13.clone.1 | convolution fusion | flops 14497087488 | bytes 17301508 | tf_op jit(solution)/shard_map/while/body/eval_jaxpr/dot_general | solution.py:33
  422.4 13.5 %cosine_multiply_fusion.2 = (f32[1536,512]{1,0:T(8,128)S(1)}, f32[1536,512]{1,0:T(8,128)S(1)}) fusion(s32[512]{0:T(512)S(1)} %iota_add_fusion.2, f32[1536]{0:T(1024)S(1)} %get-tuple-element.131, f32[1536]{0:T(1024)S(1)} %get-tuple-element.132), kind=kLoop, calls=%fused_computation.8.clone.1 | loop fusion | flops 8650752 | bytes 6305792 | tf_op jit(solution)/shard_map/while/body/eval_jaxpr/mul | solution.py:18
  435.9 33.4 %fusion.28 = f32[3072,768]{1,0:T(8,128)} fusion(f32[3072,768]{1,0:T(8,128)} %get-tuple-element.143, s32[]{:T(128)S(6)} %select_n.61, f32[3072,768]{1,0:T(8,128)} %get-tuple-element.151, f32[1536,512]{1,0:T(8,128)S(1)} %get-tuple-element.133, f32[1536,512]{1,0:T(8,128)S(1)} %get-tuple-element.134), kind=kOutput, calls=%fused_computation.13.clone.1 | convolution fusion | flops 14497087488 | bytes 17301508 | tf_op jit(solution)/shard_map/while/body/eval_jaxpr/dot_general | solution.py:33
  469.3 13.5 %cosine_multiply_fusion.2 = (f32[1536,512]{1,0:T(8,128)S(1)}, f32[1536,512]{1,0:T(8,128)S(1)}) fusion(s32[512]{0:T(512)S(1)} %iota_add_fusion.2, f32[1536]{0:T(1024)S(1)} %get-tuple-element.131, f32[1536]{0:T(1024)S(1)} %get-tuple-element.132), kind=kLoop, calls=%fused_computation.8.clone.1 | loop fusion | flops 8650752 | bytes 6305792 | tf_op jit(solution)/shard_map/while/body/eval_jaxpr/mul | solution.py:18
  482.8 33.4 %fusion.28 = f32[3072,768]{1,0:T(8,128)} fusion(f32[3072,768]{1,0:T(8,128)} %get-tuple-element.143, s32[]{:T(128)S(6)} %select_n.61, f32[3072,768]{1,0:T(8,128)} %get-tuple-element.151, f32[1536,512]{1,0:T(8,128)S(1)} %get-tuple-element.133, f32[1536,512]{1,0:T(8,128)S(1)} %get-tuple-element.134), kind=kOutput, calls=%fused_computation.13.clone.1 | convolution fusion | flops 14497087488 | bytes 17301508 | tf_op jit(solution)/shard_map/while/body/eval_jaxpr/dot_general | solution.py:33
  516.2 13.5 %cosine_multiply_fusion.2 = (f32[1536,512]{1,0:T(8,128)S(1)}, f32[1536,512]{1,0:T(8,128)S(1)}) fusion(s32[512]{0:T(512)S(1)} %iota_add_fusion.2, f32[1536]{0:T(1024)S(1)} %get-tuple-element.131, f32[1536]{0:T(1024)S(1)} %get-tuple-element.132), kind=kLoop, calls=%fused_computation.8.clone.1 | loop fusion | flops 8650752 | bytes 6305792 | tf_op jit(solution)/shard_map/while/body/eval_jaxpr/mul | solution.py:18
  529.7 33.4 %fusion.28 = f32[3072,768]{1,0:T(8,128)} fusion(f32[3072,768]{1,0:T(8,128)} %get-tuple-element.143, s32[]{:T(128)S(6)} %select_n.61, f32[3072,768]{1,0:T(8,128)} %get-tuple-element.151, f32[1536,512]{1,0:T(8,128)S(1)} %get-tuple-element.133, f32[1536,512]{1,0:T(8,128)S(1)} %get-tuple-element.134), kind=kOutput, calls=%fused_computation.13.clone.1 | convolution fusion | flops 14497087488 | bytes 17301508 | tf_op jit(solution)/shard_map/while/body/eval_jaxpr/dot_general | solution.py:33
  563.1 13.5 %cosine_multiply_fusion.2 = (f32[1536,512]{1,0:T(8,128)S(1)}, f32[1536,512]{1,0:T(8,128)S(1)}) fusion(s32[512]{0:T(512)S(1)} %iota_add_fusion.2, f32[1536]{0:T(1024)S(1)} %get-tuple-element.131, f32[1536]{0:T(1024)S(1)} %get-tuple-element.132), kind=kLoop, calls=%fused_computation.8.clone.1 | loop fusion | flops 8650752 | bytes 6305792 | tf_op jit(solution)/shard_map/while/body/eval_jaxpr/mul | solution.py:18
  576.6 33.4 %fusion.28 = f32[3072,768]{1,0:T(8,128)} fusion(f32[3072,768]{1,0:T(8,128)} %get-tuple-element.143, s32[]{:T(128)S(6)} %select_n.61, f32[3072,768]{1,0:T(8,128)} %get-tuple-element.151, f32[1536,512]{1,0:T(8,128)S(1)} %get-tuple-element.133, f32[1536,512]{1,0:T(8,128)S(1)} %get-tuple-element.134), kind=kOutput, calls=%fused_computation.13.clone.1 | convolution fusion | flops 14497087488 | bytes 17301508 | tf_op jit(solution)/shard_map/while/body/eval_jaxpr/dot_general | solution.py:33
  610.1 9.5 copy.19
  619.6 5.0 all-to-all-start.1
  624.7 0.0 reduce-scatter.2.cloned.1.call-start
  624.7 9.6 copy.20
  634.4 0.0 copy-start.1
  634.4 195.0 %all-to-all-done.1 = f32[8,384,768]{1,2,0:T(8,128)} async-done(((f32[8,384,768]{1,2,0:T(8,128)}), f32[8,384,768]{1,2,0:T(8,128)}, u32[]{:S(2)}, u32[]{:S(2)}) %all-to-all-start.1) | async-done | bytes 9437216 | tf_op jit(solution)/shard_map/all_to_all | solution.py:43
  829.4 11.2 %bitcast_multiply_fusion = f32[384,6144]{0,1:T(8,128)} fusion(f32[384,6144]{0,1:T(8,128)} %copy.20, f32[8,384,768]{1,2,0:T(8,128)} %all-to-all-done.1), kind=kLoop, calls=%fused_computation.19 | loop fusion | flops 2359296 | bytes 28311552 | tf_op jit(solution)/shard_map/mul | solution.py:44
  840.6 0.0 copy-done.1
  840.6 21.0 %fusion.16 = f32[16,384,128]{2,1,0:T(8,128)} fusion(f32[384,384,16]{0,2,1:T(8,128)} %bitcast.26, f32[384,128]{1,0:T(8,128)S(1)} %copy-done.1), kind=kOutput, calls=%fused_computation.22 | convolution fusion | flops 3623878656 | bytes 12779520 | tf_op jit(solution)/shard_map/xyz,yr->zxr/dot_general | solution.py:48
  861.6 0.0 copy-start.2
  861.6 0.0 reduce-scatter.2.cloned.1.call-update
  861.7 0.0 all-reduce.3.cloned.1.call-start
  861.7 37.0 %reduce-scatter.2.cloned.1.call-done = f32[4,384,128]{2,1,0:T(8,128)} async-done(((f32[16,384,128]{2,1,0:T(8,128)}), f32[4,384,128]{2,1,0:T(8,128)}) %reduce-scatter.2.cloned.1.call-update) | async-done | bytes 786448 | tf_op jit(solution)/shard_map/reduce_scatter | solution.py:47
  898.8 0.0 copy-done
  898.8 2.6 convolution_bitcast_fusion
  901.3 1.0 copy.23
  902.3 0.0 all-reduce.3.cloned.1.call-update
  902.3 0.0 copy-done.2
  902.3 0.6 dynamic-slice
  903.6 71.6 %all-reduce.3.cloned.1.call-done = f32[4,256,128]{2,0,1:T(4,128)} async-done(((f32[4,256,128]{2,0,1:T(4,128)}), f32[4,256,128]{2,0,1:T(4,128)}) %all-reduce.3.cloned.1.call-update) | async-done | bytes 524304
  975.2 0.8 constant_dynamic-slice_fusion
  976.1 0.6 copy.24
  (12 shorter events, 0.0 us)
Async XLA Ops:
  7.2 891.6 %copy-start = (f32[384,256]{1,0:T(8,128)S(1)}, f32[384,256]{1,0:T(8,128)}, u32[]{:S(2)}) copy-start(f32[384,256]{1,0:T(8,128)} %param.9) | copy-start | bytes 1179652
  25.6 280.4 %all-to-all-start = ((f32[2,192,6144]{1,0,2:T(2,128)}), f32[2,192,6144]{1,0,2:T(2,128)}, u32[]{:S(2)}, u32[]{:S(2)}) async-start(f32[2,192,6144]{1,0,2:T(2,128)} %copy.17), calls=%async_computation | async-start | bytes 25165824 | tf_op jit(solution)/shard_map/all_to_all | solution.py:25
  619.6 209.8 %all-to-all-start.1 = ((f32[8,384,768]{1,2,0:T(8,128)}), f32[8,384,768]{1,2,0:T(8,128)}, u32[]{:S(2)}, u32[]{:S(2)}) async-start(f32[8,384,768]{1,2,0:T(8,128)} %copy.19), calls=%async_computation.1 | async-start | bytes 18874368 | tf_op jit(solution)/shard_map/all_to_all | solution.py:43
  624.7 274.1 %reduce-scatter.2.cloned.1.call-start = ((), (), s32[]{:S(2)}) async-start(), calls=%async_computation.3 | async-start | bytes 3932160 | tf_op jit(solution)/shard_map/reduce_scatter | solution.py:47
  634.4 206.3 %copy-start.1 = (f32[384,128]{1,0:T(8,128)S(1)}, f32[384,128]{1,0:T(8,128)}, u32[]{:S(2)}) copy-start(f32[384,128]{1,0:T(8,128)} %param.8) | copy-start | bytes 589828
  861.6 40.7 %copy-start.2 = (u32[32]{0:T(128)S(1)}, u32[32]{0:T(128)}, u32[]{:S(2)}) copy-start(u32[32]{0:T(128)} %constant.99) | copy-start | bytes 388
  861.7 113.6 %all-reduce.3.cloned.1.call-start = ((), (), s32[]{:S(2)}) async-start(), calls=%async_computation.4 | async-start | bytes 1048576
Sparse Core Ops, SparseCore 0:
  861.8 36.9 reduce-scatter.1
  902.5 72.7 all-reduce.2
where the time goes:
time: 985 us; the launch traced here: 984 us
  waiting for transfers between devices  577 us (59%)
  matrix products  224 us (23%)
  other arithmetic  92.3 us (9%)
  local copies, waits for them, and re-layouts  63.2 us (6%)
  between operations  14.7 us (1%)
  starting transfers between devices  12.4 us (1%)
    all_to_all x1, waiting for transfers between devices, body(): lax.all_to_all(spectrum, 'px', split_axis=2, concat_axis=1, tiled=True)  273 us
    dot_general x6, matrix products, fill_block(): lax.dot_general(synth_table(first_x, block_width), stacked_modes, (((0,),...  200 us
    all_to_all x1, waiting for transfers between devices, body(): lax.all_to_all(velocity, 'px', split_axis=0, concat_axis=1, tiled=True)  195 us
    mul x6, other arithmetic, synth_table(): weight * jnp.cos(angle)  81 us
    unnamed x3, waiting for transfers between devices  71.7 us
    reduce_scatter x1, waiting for transfers between devices, body(): lax.psum_scatter(jnp.einsum('xyz,yr->zxr', rows, factor_y, precision=lax....  37 us
    unnamed x11, local copies, waits for them, and re-layouts  30.1 us
    dot_general x1, matrix products, body(): jnp.einsum('xyz,yr->zxr', rows, factor_y, precision=lax.Precision.HIGHEST)  21 us
  transfers between devices with their start and end apart: 4, of which 4 were waited for; matrix products, arithmetic and copies ran while one was open for 1% of the time, Pallas kernels for 0%

commit v1 on v0

--- a/solution.py
+++ b/solution.py
@@ -22,7 +22,9 @@
     x_local = concentration.shape[0]
     line_total = concentration.shape[1]
     y_local = line_total // NZ
-    pencil_modes = lax.all_to_all(spectrum, "px", split_axis=2, concat_axis=1, tiled=True)
+    pieces = jnp.split(spectrum, lax.axis_size("px"), axis=2)
+    received = lax.all_to_all(jnp.stack(pieces), "px", 0, 0)
+    pencil_modes = jnp.concatenate(received, axis=1)
     line_count = pencil_modes.shape[2]
     stacked_modes = pencil_modes.reshape(2 * KX, line_count)
     block_width = 512

time: 985 us -> 908 us (0.922)
  waiting for transfers between devices: 577 us -> 509 us
    all_to_all x1, waiting for transfers between devices: 273 us -> 206 us  [body(): received = lax.all_to_all(jnp.stack(pieces), 'px', 0, 0)]
    all_to_all x1 -> x0, local copies, waits for them, and re-layouts: 18.3 us -> none  [body(): lax.all_to_all(spectrum, 'px', split_axis=2, concat_axis=1, tiled=True)]
    unnamed x11 -> x17, local copies, waits for them, and re-layouts: 30.1 us -> 28.5 us
where the time goes in v1:
time: 908 us; the launch traced here: 907 us
  waiting for transfers between devices  509 us (56%)
  matrix products  224 us (25%)
  other arithmetic  92.3 us (10%)
  local copies, waits for them, and re-layouts  53.9 us (6%)
  between operations  14.7 us (2%)
  starting transfers between devices  12.4 us (1%)
    all_to_all x1, waiting for transfers between devices, body(): received = lax.all_to_all(jnp.stack(pieces), 'px', 0, 0)  206 us
    dot_general x6, matrix products, fill_block(): lax.dot_general(synth_table(first_x, block_width), stacked_modes, (((0,),...  200 us
    all_to_all x1, waiting for transfers between devices, body(): lax.all_to_all(velocity, 'px', split_axis=0, concat_axis=1, tiled=True)  195 us
    mul x6, other arithmetic, synth_table(): weight * jnp.cos(angle)  81 us
    unnamed x3, waiting for transfers between devices  71.7 us
    reduce_scatter x1, waiting for transfers between devices, body(): lax.psum_scatter(jnp.einsum('xyz,yr->zxr', rows, factor_y, precision=lax....  37 us
    unnamed x17, local copies, waits for them, and re-layouts  28.5 us
    dot_general x1, matrix products, body(): jnp.einsum('xyz,yr->zxr', rows, factor_y, precision=lax.Precision.HIGHEST)  21 us
  transfers between devices with their start and end apart: 4, of which 4 were waited for; matrix products, arithmetic and copies ran while one was open for 1% of the time, Pallas kernels for 0%

profile of v1, /device:TPU:0, one launch (start us, length us, event | category | flops | bytes accessed | tf_op | source)
XLA Modules:
  0.0 906.9 jit_solution(5710014350999524674)
XLA Ops:
  7.2 0.0 copy-start
  7.2 2.4 bitcast_dynamic-update-slice_fusion.7
  9.6 2.4 bitcast_dynamic-update-slice_fusion.6
  12.0 2.4 bitcast_dynamic-update-slice_fusion.5
  14.4 2.4 bitcast_dynamic-update-slice_fusion.4
  16.7 2.4 bitcast_dynamic-update-slice_fusion.3
  19.2 2.4 bitcast_dynamic-update-slice_fusion.2
  21.5 2.4 bitcast_dynamic-update-slice_fusion.1
  23.9 2.5 bitcast_dynamic-update-slice_fusion
  26.4 7.3 all-to-all-start
  33.7 205.6 %all-to-all-done = f32[8,2,192,768]{3,2,1,0:T(8,128)} async-done(((f32[8,2,192,768]{3,2,1,0:T(8,128)}), f32[8,2,192,768]{3,2,1,0:T(8,128)}, u32[]{:S(2)}, u32[]{:S(2)}) %all-to-all-start) | async-done | bytes 9437216 | tf_op jit(solution)/shard_map/all_to_all | solution.py:26
  239.3 8.2 copy.17
  247.5 4.3 broadcast_in_dim.15
  251.8 281.6 %while.15 = (s32[]{:T(128)}, f32[3072,768]{1,0:T(8,128)}, f32[3072,768]{1,0:T(8,128)}, s32[]{:T(128)}, s32[]{:T(128)}, /*index=5*/s32[]{:T(128)}, s32[]{:T(128)}) while((s32[]{:T(128)}, f32[3072,768]{1,0:T(8,128)}, f32[3072,768]{1,0:T(8,128)}, s32[]{:T(128)}, s32[]{:T(128)}, /*index=5*/s32[]{:T(128)}, s32[]{:T(128)}) %tuple.56), condition=%wide.region_1.2_spmd, body=%wide.region_0.1_spmd.sunk | while | flops 14505745408 | bytes 23621764 | solution.py:44
  251.8 13.5 %cosine_multiply_fusion.2 = (f32[1536,512]{1,0:T(8,128)S(1)}, f32[1536,512]{1,0:T(8,128)S(1)}) fusion(s32[512]{0:T(512)S(1)} %iota_add_fusion.2, f32[1536]{0:T(1024)S(1)} %get-tuple-element.131, f32[1536]{0:T(1024)S(1)} %get-tuple-element.132), kind=kLoop, calls=%fused_computation.8.clone.1 | loop fusion | flops 8650752 | bytes 6305792 | tf_op jit(solution)/shard_map/while/body/eval_jaxpr/mul | solution.py:18
  265.3 33.4 %fusion.28 = f32[3072,768]{1,0:T(8,128)} fusion(f32[3072,768]{1,0:T(8,128)} %get-tuple-element.143, s32[]{:T(128)S(6)} %select_n.61, f32[3072,768]{1,0:T(8,128)} %get-tuple-element.151, f32[1536,512]{1,0:T(8,128)S(1)} %get-tuple-element.133, f32[1536,512]{1,0:T(8,128)S(1)} %get-tuple-element.134), kind=kOutput, calls=%fused_computation.13.clone.1 | convolution fusion | flops 14497087488 | bytes 17301508 | tf_op jit(solution)/shard_map/while/body/eval_jaxpr/dot_general | solution.py:35
  298.7 13.5 %cosine_multiply_fusion.2 = (f32[1536,512]{1,0:T(8,128)S(1)}, f32[1536,512]{1,0:T(8,128)S(1)}) fusion(s32[512]{0:T(512)S(1)} %iota_add_fusion.2, f32[1536]{0:T(1024)S(1)} %get-tuple-element.131, f32[1536]{0:T(1024)S(1)} %get-tuple-element.132), kind=kLoop, calls=%fused_computation.8.clone.1 | loop fusion | flops 8650752 | bytes 6305792 | tf_op jit(solution)/shard_map/while/body/eval_jaxpr/mul | solution.py:18
  312.2 33.4 %fusion.28 = f32[3072,768]{1,0:T(8,128)} fusion(f32[3072,768]{1,0:T(8,128)} %get-tuple-element.143, s32[]{:T(128)S(6)} %select_n.61, f32[3072,768]{1,0:T(8,128)} %get-tuple-element.151, f32[1536,512]{1,0:T(8,128)S(1)} %get-tuple-element.133, f32[1536,512]{1,0:T(8,128)S(1)} %get-tuple-element.134), kind=kOutput, calls=%fused_computation.13.clone.1 | convolution fusion | flops 14497087488 | bytes 17301508 | tf_op jit(solution)/shard_map/while/body/eval_jaxpr/dot_general | solution.py:35
  345.7 13.5 %cosine_multiply_fusion.2 = (f32[1536,512]{1,0:T(8,128)S(1)}, f32[1536,512]{1,0:T(8,128)S(1)}) fusion(s32[512]{0:T(512)S(1)} %iota_add_fusion.2, f32[1536]{0:T(1024)S(1)} %get-tuple-element.131, f32[1536]{0:T(1024)S(1)} %get-tuple-element.132), kind=kLoop, calls=%fused_computation.8.clone.1 | loop fusion | flops 8650752 | bytes 6305792 | tf_op jit(solution)/shard_map/while/body/eval_jaxpr/mul | solution.py:18
  359.2 33.4 %fusion.28 = f32[3072,768]{1,0:T(8,128)} fusion(f32[3072,768]{1,0:T(8,128)} %get-tuple-element.143, s32[]{:T(128)S(6)} %select_n.61, f32[3072,768]{1,0:T(8,128)} %get-tuple-element.151, f32[1536,512]{1,0:T(8,128)S(1)} %get-tuple-element.133, f32[1536,512]{1,0:T(8,128)S(1)} %get-tuple-element.134), kind=kOutput, calls=%fused_computation.13.clone.1 | convolution fusion | flops 14497087488 | bytes 17301508 | tf_op jit(solution)/shard_map/while/body/eval_jaxpr/dot_general | solution.py:35
  392.6 13.5 %cosine_multiply_fusion.2 = (f32[1536,512]{1,0:T(8,128)S(1)}, f32[1536,512]{1,0:T(8,128)S(1)}) fusion(s32[512]{0:T(512)S(1)} %iota_add_fusion.2, f32[1536]{0:T(1024)S(1)} %get-tuple-element.131, f32[1536]{0:T(1024)S(1)} %get-tuple-element.132), kind=kLoop, calls=%fused_computation.8.clone.1 | loop fusion | flops 8650752 | bytes 6305792 | tf_op jit(solution)/shard_map/while/body/eval_jaxpr/mul | solution.py:18
  406.2 33.4 %fusion.28 = f32[3072,768]{1,0:T(8,128)} fusion(f32[3072,768]{1,0:T(8,128)} %get-tuple-element.143, s32[]{:T(128)S(6)} %select_n.61, f32[3072,768]{1,0:T(8,128)} %get-tuple-element.151, f32[1536,512]{1,0:T(8,128)S(1)} %get-tuple-element.133, f32[1536,512]{1,0:T(8,128)S(1)} %get-tuple-element.134), kind=kOutput, calls=%fused_computation.13.clone.1 | convolution fusion | flops 14497087488 | bytes 17301508 | tf_op jit(solution)/shard_map/while/body/eval_jaxpr/dot_general | solution.py:35
  439.6 13.5 %cosine_multiply_fusion.2 = (f32[1536,512]{1,0:T(8,128)S(1)}, f32[1536,512]{1,0:T(8,128)S(1)}) fusion(s32[512]{0:T(512)S(1)} %iota_add_fusion.2, f32[1536]{0:T(1024)S(1)} %get-tuple-element.131, f32[1536]{0:T(1024)S(1)} %get-tuple-element.132), kind=kLoop, calls=%fused_computation.8.clone.1 | loop fusion | flops 8650752 | bytes 6305792 | tf_op jit(solution)/shard_map/while/body/eval_jaxpr/mul | solution.py:18
  453.1 33.4 %fusion.28 = f32[3072,768]{1,0:T(8,128)} fusion(f32[3072,768]{1,0:T(8,128)} %get-tuple-element.143, s32[]{:T(128)S(6)} %select_n.61, f32[3072,768]{1,0:T(8,128)} %get-tuple-element.151, f32[1536,512]{1,0:T(8,128)S(1)} %get-tuple-element.133, f32[1536,512]{1,0:T(8,128)S(1)} %get-tuple-element.134), kind=kOutput, calls=%fused_computation.13.clone.1 | convolution fusion | flops 14497087488 | bytes 17301508 | tf_op jit(solution)/shard_map/while/body/eval_jaxpr/dot_general | solution.py:35
  486.5 13.5 %cosine_multiply_fusion.2 = (f32[1536,512]{1,0:T(8,128)S(1)}, f32[1536,512]{1,0:T(8,128)S(1)}) fusion(s32[512]{0:T(512)S(1)} %iota_add_fusion.2, f32[1536]{0:T(1024)S(1)} %get-tuple-element.131, f32[1536]{0:T(1024)S(1)} %get-tuple-element.132), kind=kLoop, calls=%fused_computation.8.clone.1 | loop fusion | flops 8650752 | bytes 6305792 | tf_op jit(solution)/shard_map/while/body/eval_jaxpr/mul | solution.py:18
  500.0 33.4 %fusion.28 = f32[3072,768]{1,0:T(8,128)} fusion(f32[3072,768]{1,0:T(8,128)} %get-tuple-element.143, s32[]{:T(128)S(6)} %select_n.61, f32[3072,768]{1,0:T(8,128)} %get-tuple-element.151, f32[1536,512]{1,0:T(8,128)S(1)} %get-tuple-element.133, f32[1536,512]{1,0:T(8,128)S(1)} %get-tuple-element.134), kind=kOutput, calls=%fused_computation.13.clone.1 | convolution fusion | flops 14497087488 | bytes 17301508 | tf_op jit(solution)/shard_map/while/body/eval_jaxpr/dot_general | solution.py:35
  533.4 9.5 %copy.18 = f32[8,384,768]{1,2,0:T(8,128)} copy(f32[8,384,768]{2,1,0:T(8,128)} %bitcast.41) | data formatting | bytes 18874368 | tf_op jit(solution)/shard_map/all_to_all | solution.py:45
  543.0 5.0 all-to-all-start.1
  548.0 0.0 reduce-scatter.2.cloned.1.call-start
  548.1 9.6 %copy.19 = f32[384,6144]{0,1:T(8,128)} copy(f32[384,6144]{1,0:T(8,128)} %param.7) | data formatting | bytes 18874368 | tf_op args[1]
  557.7 0.0 copy-start.1
  557.7 195.0 %all-to-all-done.1 = f32[8,384,768]{1,2,0:T(8,128)} async-done(((f32[8,384,768]{1,2,0:T(8,128)}), f32[8,384,768]{1,2,0:T(8,128)}, u32[]{:S(2)}, u32[]{:S(2)}) %all-to-all-start.1) | async-done | bytes 9437216 | tf_op jit(solution)/shard_map/all_to_all | solution.py:45
  752.7 11.2 %bitcast_multiply_fusion = f32[384,6144]{0,1:T(8,128)} fusion(f32[384,6144]{0,1:T(8,128)} %copy.19, f32[8,384,768]{1,2,0:T(8,128)} %all-to-all-done.1), kind=kLoop, calls=%fused_computation.19 | loop fusion | flops 2359296 | bytes 28311552 | tf_op jit(solution)/shard_map/mul | solution.py:46
  764.0 0.0 copy-done.1
  764.0 0.0 copy-start.2
  764.0 21.0 %fusion.16 = f32[16,384,128]{2,1,0:T(8,128)} fusion(f32[384,384,16]{0,2,1:T(8,128)} %bitcast.40, f32[384,128]{1,0:T(8,128)S(1)} %copy-done.1), kind=kOutput, calls=%fused_computation.22 | convolution fusion | flops 3623878656 | bytes 12779520 | tf_op jit(solution)/shard_map/xyz,yr->zxr/dot_general | solution.py:50
  785.0 0.0 reduce-scatter.2.cloned.1.call-update
  785.0 0.0 all-reduce.3.cloned.1.call-start
  785.1 37.0 %reduce-scatter.2.cloned.1.call-done = f32[4,384,128]{2,1,0:T(8,128)} async-done(((f32[16,384,128]{2,1,0:T(8,128)}), f32[4,384,128]{2,1,0:T(8,128)}) %reduce-scatter.2.cloned.1.call-update) | async-done | bytes 786448 | tf_op jit(solution)/shard_map/reduce_scatter | solution.py:49
  822.1 0.0 copy-done
  822.1 2.6 convolution_bitcast_fusion
  824.7 1.0 copy.22
  825.7 0.0 all-reduce.3.cloned.1.call-update
  825.7 0.0 copy-done.2
  825.7 0.6 dynamic-slice
  826.9 71.6 %all-reduce.3.cloned.1.call-done = f32[4,256,128]{2,0,1:T(4,128)} async-done(((f32[4,256,128]{2,0,1:T(4,128)}), f32[4,256,128]{2,0,1:T(4,128)}) %all-reduce.3.cloned.1.call-update) | async-done | bytes 524304
  898.6 0.8 constant_dynamic-slice_fusion
  899.4 0.6 copy.23
  (12 shorter events, 0.0 us)
Async XLA Ops:
  7.2 814.9 %copy-start = (f32[384,256]{1,0:T(8,128)S(1)}, f32[384,256]{1,0:T(8,128)}, u32[]{:S(2)}) copy-start(f32[384,256]{1,0:T(8,128)} %param.9) | copy-start | bytes 1179652
  26.4 212.9 %all-to-all-start = ((f32[8,2,192,768]{3,2,1,0:T(8,128)}), f32[8,2,192,768]{3,2,1,0:T(8,128)}, u32[]{:S(2)}, u32[]{:S(2)}) async-start(f32[8,2,192,768]{3,2,1,0:T(8,128)} %bitcast_dynamic-update-slice_fusion), calls=%async_computation | async-start | bytes 18874368 | tf_op jit(solution)/shard_map/all_to_all | solution.py:26
  543.0 209.8 %all-to-all-start.1 = ((f32[8,384,768]{1,2,0:T(8,128)}), f32[8,384,768]{1,2,0:T(8,128)}, u32[]{:S(2)}, u32[]{:S(2)}) async-start(f32[8,384,768]{1,2,0:T(8,128)} %copy.18), calls=%async_computation.1 | async-start | bytes 18874368 | tf_op jit(solution)/shard_map/all_to_all | solution.py:45
  548.0 274.1 %reduce-scatter.2.cloned.1.call-start = ((), (), s32[]{:S(2)}) async-start(), calls=%async_computation.3 | async-start | bytes 3932160 | tf_op jit(solution)/shard_map/reduce_scatter | solution.py:49
  557.7 206.3 %copy-start.1 = (f32[384,128]{1,0:T(8,128)S(1)}, f32[384,128]{1,0:T(8,128)}, u32[]{:S(2)}) copy-start(f32[384,128]{1,0:T(8,128)} %param.8) | copy-start | bytes 589828
  764.0 61.7 %copy-start.2 = (u32[32]{0:T(128)S(1)}, u32[32]{0:T(128)}, u32[]{:S(2)}) copy-start(u32[32]{0:T(128)} %constant.99) | copy-start | bytes 388
  785.0 113.6 %all-reduce.3.cloned.1.call-start = ((), (), s32[]{:S(2)}) async-start(), calls=%async_computation.4 | async-start | bytes 1048576
Sparse Core Ops, SparseCore 0:
  785.1 36.9 reduce-scatter.1
  825.8 72.7 all-reduce.2
